TPU v7x, 32 devices: a whole 2x2x4 slice. The times are simulated.
32 devices in a mesh: groups: 2 (over y), expert: 4 (over z), dp: 4 (over x, core).
Axes of the slice: x: 2, y: 2, z: 4, core: 2. Of those that a mesh axis runs over, the one named last changes fastest.
Arguments:
- tokens: bfloat16 [4096, 2048], P(('groups', 'expert', 'dp')), parts along dimension 0, may hold values from -6 to 6
- cotangent: bfloat16 [4096, 2048], P(('groups', 'expert', 'dp')), parts along dimension 0, may hold values from -1.5 to 1.5
- expert_ids: int32 [4096, 8], P(('groups', 'expert', 'dp')), parts along dimension 0, may hold values from 0 to 127, all different within a row; in each aligned block of 128 rows (0 to 127, 128 to 255, ...) at most 16 rows name the same one
- gate_probs: float32 [4096, 8], P(('groups', 'expert', 'dp')), parts along dimension 0, may hold values from 0.05 to 0.6
- w_gate: bfloat16 [4, 2048, 384], P('expert', 'dp'), may hold values from -0.125 to 0.125
- w_up: bfloat16 [4, 2048, 384], P('expert', 'dp'), may hold values from -0.125 to 0.125
- w_down: bfloat16 [4, 384, 2048], P('expert', None, 'dp'), may hold values from -0.3125 to 0.3125
Outputs:
- mixed: bfloat16 [4096, 2048], P(('groups', 'expert', 'dp')), parts along dimension 0
- grad_tokens: bfloat16 [4096, 2048], P(('groups', 'expert', 'dp')), parts along dimension 0
- grad_gates: float32 [4096, 8], P(('groups', 'expert', 'dp')), parts along dimension 0
- grad_w_gate: bfloat16 [8, 2048, 384], P(('groups', 'expert'), 'dp'), parts along dimension 0
- grad_w_up: bfloat16 [8, 2048, 384], P(('groups', 'expert'), 'dp'), parts along dimension 0
- grad_w_down: bfloat16 [8, 384, 2048], P(('groups', 'expert'), None, 'dp'), parts along dimension 0
There are 2 independent parts, one for each index of `groups`. A program takes and returns all parts, laid end to end along the dimension named above; an argument that names none is the same for every part. Nothing has to cross between parts.
Inputs may be any that keep to these rules, and one draw needn't show every extreme that they name: `expert_ids`: each token names 8 different experts. In the rows of one device (aligned blocks of 128 tokens) no expert is named more than 16 times, and in every draw some expert is named exactly 16 times in some block.
All inputs are finite; a program needn't handle non-finite values.
Results may differ from a plain program's by a relative error of at most 0.0058.
Values may be sent and summed in bfloat16 or wider, within the bound.
No kernel may reach another device: no remote copies, remote signals or barrier semaphores. Data moves between devices by JAX's collectives and lax.ppermute only.
A program may use at most 128 MiB of HBM per device.

v0:
```python
import jax
import jax.numpy as jnp
from jax import lax
from jax.sharding import PartitionSpec as P

EXPERTS = 128


def dot_last(left, right):
    return lax.dot_general(
        left, right, (((1,), (1,)), ((), ())), preferred_element_type=jnp.float32
    )


def expert_rows(rows_x, rows_dy, gate_full, up_full, down_full):
    gate_part = jnp.dot(rows_x, gate_full, preferred_element_type=jnp.float32)
    up_part = jnp.dot(rows_x, up_full, preferred_element_type=jnp.float32)
    sigmoid_gate = jax.nn.sigmoid(gate_part)
    activated = gate_part * sigmoid_gate
    hidden = (activated * up_part).astype(jnp.bfloat16)
    expert_out = jnp.dot(hidden, down_full, preferred_element_type=jnp.float32).astype(jnp.bfloat16)
    back_hidden = dot_last(rows_dy, down_full)
    d_gate = (
        back_hidden * up_part * sigmoid_gate * (1.0 + gate_part * (1.0 - sigmoid_gate))
    ).astype(jnp.bfloat16)
    d_up = (back_hidden * activated).astype(jnp.bfloat16)
    d_rows = (dot_last(d_gate, gate_full) + dot_last(d_up, up_full)).astype(jnp.bfloat16)
    return (hidden, expert_out, d_gate, d_up, d_rows)


def on_device(tokens, cotangent, expert_ids, gate_probs, w_gate, w_up, w_down):
    expert_count = lax.axis_size("expert")
    dp_count = lax.axis_size("dp")
    token_rows, model_width = tokens.shape
    top_count = expert_ids.shape[1]
    slice_width = w_gate.shape[1]
    hidden_width = w_gate.shape[2]
    capacity = 2 * token_rows * top_count // EXPERTS
    slot_total = expert_count * capacity
    flat_ids = expert_ids.reshape(-1)
    onehot = (flat_ids[:, None] == jnp.arange(EXPERTS, dtype=jnp.int32)[None, :]).astype(jnp.int32)
    running = jnp.cumsum(onehot, axis=0)
    slot_index = jnp.sum(running * onehot, axis=1) - 1
    in_wave = flat_ids < expert_count
    position = jnp.where(in_wave, flat_ids * capacity + slot_index, slot_total)
    matched = position[:, None] == jnp.arange(slot_total, dtype=jnp.int32)[None, :]
    owner_row = jnp.arange(token_rows * top_count, dtype=jnp.int32) // top_count
    source = jnp.sum(jnp.where(matched, owner_row[:, None], 0), axis=0)
    filled = jnp.any(matched, axis=0)
    zero_value = jnp.zeros((), jnp.bfloat16)
    send_x = jnp.where(filled[:, None], jnp.take(tokens, source, axis=0), zero_value).reshape(
        expert_count, capacity, model_width
    )
    send_dy = jnp.where(filled[:, None], jnp.take(cotangent, source, axis=0), zero_value).reshape(
        expert_count, capacity, model_width
    )
    gate_full, up_full, down_full = (
        lax.all_gather(w_gate, "dp", axis=1, tiled=True),
        lax.all_gather(w_up, "dp", axis=1, tiled=True),
        lax.all_gather(w_down, "dp", axis=2, tiled=True),
    )
    gate_full = gate_full[0]
    up_full = up_full[0]
    down_full = down_full[0]
    got_x, got_dy = (
        lax.all_to_all(send_x, "expert", split_axis=0, concat_axis=0, tiled=True),
        lax.all_to_all(send_dy, "expert", split_axis=0, concat_axis=0, tiled=True),
    )
    rows_x = got_x.reshape(slot_total, model_width)
    rows_dy = got_dy.reshape(slot_total, model_width)
    hidden, expert_out, d_gate, d_up, d_rows = expert_rows(
        rows_x, rows_dy, gate_full, up_full, down_full
    )
    back_out, back_rows = (
        lax.all_to_all(
            expert_out.reshape(expert_count, capacity, model_width),
            "expert",
            split_axis=0,
            concat_axis=0,
            tiled=True,
        ),
        lax.all_to_all(
            d_rows.reshape(expert_count, capacity, model_width),
            "expert",
            split_axis=0,
            concat_axis=0,
            tiled=True,
        ),
    )
    back_out = back_out.reshape(slot_total, model_width)
    back_rows = back_rows.reshape(slot_total, model_width)
    matched_three = matched.reshape(token_rows, top_count, slot_total)
    weight_table = jnp.sum(jnp.where(matched_three, gate_probs[:, :, None], 0.0), axis=1)
    mixed = jnp.dot(
        weight_table, back_out.astype(jnp.float32), precision=lax.Precision.HIGHEST
    ).astype(jnp.bfloat16)
    grad_tokens = jnp.dot(
        weight_table, back_rows.astype(jnp.float32), precision=lax.Precision.HIGHEST
    ).astype(jnp.bfloat16)
    inner_table = dot_last(cotangent, back_out)
    grad_gates = jnp.sum(jnp.where(matched_three, inner_table[:, None, :], 0.0), axis=2)
    local_gate = jnp.einsum("sd,sf->df", rows_x, d_gate, preferred_element_type=jnp.float32).astype(
        jnp.bfloat16
    )
    local_up = jnp.einsum("sd,sf->df", rows_x, d_up, preferred_element_type=jnp.float32).astype(
        jnp.bfloat16
    )
    local_down = jnp.einsum(
        "sd,sf->df", rows_dy, hidden, preferred_element_type=jnp.float32
    ).astype(jnp.bfloat16)
    got_gate, got_up, got_down = (
        lax.all_to_all(
            local_gate.reshape(dp_count, slice_width, hidden_width),
            "dp",
            split_axis=0,
            concat_axis=0,
            tiled=True,
        ),
        lax.all_to_all(
            local_up.reshape(dp_count, slice_width, hidden_width),
            "dp",
            split_axis=0,
            concat_axis=0,
            tiled=True,
        ),
        lax.all_to_all(
            local_down.reshape(dp_count, slice_width, hidden_width),
            "dp",
            split_axis=0,
            concat_axis=0,
            tiled=True,
        ),
    )
    grad_w_gate = jnp.sum(got_gate.astype(jnp.float32), axis=0).astype(jnp.bfloat16)[None]
    grad_w_up = jnp.sum(got_up.astype(jnp.float32), axis=0).astype(jnp.bfloat16)[None]
    grad_w_down = jnp.sum(got_down.astype(jnp.float32), axis=0).T.astype(jnp.bfloat16)[None]
    return (mixed, grad_tokens, grad_gates, grad_w_gate, grad_w_up, grad_w_down)


def solution(mesh):
    in_specs = (
        P(("groups", "expert", "dp"), None),
        P(("groups", "expert", "dp"), None),
        P(("groups", "expert", "dp"), None),
        P(("groups", "expert", "dp"), None),
        P("expert", "dp", None),
        P("expert", "dp", None),
        P("expert", None, "dp"),
    )
    out_specs = (
        P(("groups", "expert", "dp"), None),
        P(("groups", "expert", "dp"), None),
        P(("groups", "expert", "dp"), None),
        P(("groups", "expert"), "dp", None),
        P(("groups", "expert"), "dp", None),
        P(("groups", "expert"), None, "dp"),
    )
    return jax.shard_map(
        on_device, mesh=mesh, in_specs=in_specs, out_specs=out_specs, check_vma=False
    )
```

profile of v0, /device:TPU:0, one launch (start us, length us, event | category | flops | bytes accessed | tf_op | source)
XLA Modules:
  0.0 183.9 jit_solution(1787334633764432873)
XLA Ops:
  9.4 0.8 copy.47
  11.4 0.7 gather_fusion.1
  13.1 0.8 select_select_fusion
  13.9 15.0 %all_to_all.35 = bf16[4,16,2048]{2,1,0:T(8,128)(2,1)S(1)} all-to-all(bf16[4,16,2048]{2,1,0:T(8,128)(2,1)S(1)} %bitcast.74), channel_id=1, replica_groups=mesh['groups'=2,'expert'=4,'dp'=4] {'expert'}, dimensions={0} | all-to-all | bytes 524288 | tf_op jit(solution)/shard_map/all_to_all | solution.py:66
  28.9 3.4 %all-to-all-start.2 = ((bf16[4,16,2048]{2,1,0:T(8,128)(2,1)}), bf16[4,16,2048]{2,1,0:T(8,128)(2,1)S(1)}, u32[]{:S(2)}, u32[]{:S(2)}) async-start(bf16[4,16,2048]{2,1,0:T(8,128)(2,1)} %bitcast.10), calls=%async_computation.2 | async-start | bytes 524288 | tf_op jit(solution)/shard_map/all_to_all | solution.py:67
  32.3 1.8 fusion.9
  34.1 19.1 %all-gather.6.cloned.1.call-done = bf16[1,2048,384]{2,1,0:T(8,128)(2,1)} async-done(((bf16[1,512,384]{2,1,0:T(8,128)(2,1)}), bf16[1,2048,384]{2,1,0:T(8,128)(2,1)}) %all-gather.6.cloned.1.call-update) | async-done | bytes 1572880 | tf_op jit(solution)/shard_map/all_gather | solution.py:59
  53.2 1.8 fusion.5
  55.0 19.5 %all-gather.8.cloned.1.call-done = bf16[1,384,2048]{2,1,0:T(8,128)(2,1)} async-done(((bf16[1,384,512]{2,1,0:T(8,128)(2,1)}), bf16[1,384,2048]{2,1,0:T(8,128)(2,1)}) %all-gather.8.cloned.1.call-update) | async-done | bytes 1572880 | tf_op jit(solution)/shard_map/all_gather | solution.py:60
  74.5 2.1 %multiply_convert_fusion = (bf16[64,384]{1,0:T(8,128)(2,1)S(1)}, bf16[64,384]{1,0:T(8,128)(2,1)S(1)}, bf16[64,384]{1,0:T(8,128)(2,1)S(1)}) fusion(f32[64,384]{1,0:T(8,128)S(1)} %fusion.9, f32[64,384]{1,0:T(8,128)S(1)} %fusion.5, bf16[64,2048]{1,0:T(8,128)(2,1)S(1)} %bitcast.70, bf16[1,384,2048]{2,1,0:T(8,128)(2,1)} %all-gather.8.cloned.1.call-done), kind=kOutput, calls=%fused_computation.37 | convolution fusion | flops 101031936 | bytes 2179072 | tf_op jit(solution)/shard_map/dot_general | solution.py:10
  76.6 1.1 convolution_convert_fusion.5
  77.7 4.7 %all-to-all-start.1 = ((bf16[4,16,2048]{2,1,0:T(8,128)(2,1)}), bf16[4,16,2048]{2,1,0:T(8,128)(2,1)S(1)}, u32[]{:S(2)}, u32[]{:S(2)}) async-start(bf16[4,16,2048]{2,1,0:T(8,128)(2,1)} %bitcast.8), calls=%async_computation.1 | async-start | bytes 524288 | tf_op jit(solution)/shard_map/all_to_all | solution.py:75
  82.5 2.0 %fusion.7 = f32[64,2048]{1,0:T(8,128)S(1)} fusion(bf16[64,384]{1,0:T(8,128)(2,1)S(1)} %get-tuple-element.28, bf16[1,2048,384]{2,1,0:T(8,128)(2,1)} %all-gather.4.cloned.1.call-done), kind=kOutput, calls=%fused_computation.16 | convolution fusion | flops 100663296 | bytes 2146304 | tf_op jit(solution)/shard_map/dot_general | solution.py:10
  84.5 1.3 fusion
  85.8 6.0 %all-to-all-done.1 = bf16[4,16,2048]{2,1,0:T(8,128)(2,1)S(1)} async-done(((bf16[4,16,2048]{2,1,0:T(8,128)(2,1)}), bf16[4,16,2048]{2,1,0:T(8,128)(2,1)S(1)}, u32[]{:S(2)}, u32[]{:S(2)}) %all-to-all-start.1) | async-done | bytes 262176 | tf_op jit(solution)/shard_map/all_to_all | solution.py:75
  91.8 3.4 %all-to-all-start.3 = ((bf16[4,16,2048]{2,1,0:T(8,128)(2,1)}), bf16[4,16,2048]{2,1,0:T(8,128)(2,1)S(1)}, u32[]{:S(2)}, u32[]{:S(2)}) async-start(bf16[4,16,2048]{2,1,0:T(8,128)(2,1)} %bitcast.12), calls=%async_computation.3 | async-start | bytes 524288 | tf_op jit(solution)/shard_map/all_to_all | solution.py:82
  95.2 1.8 convolution_convert_fusion.2
  97.0 5.1 %all-to-all-done.3 = bf16[4,16,2048]{2,1,0:T(8,128)(2,1)S(1)} async-done(((bf16[4,16,2048]{2,1,0:T(8,128)(2,1)}), bf16[4,16,2048]{2,1,0:T(8,128)(2,1)S(1)}, u32[]{:S(2)}, u32[]{:S(2)}) %all-to-all-start.3) | async-done | bytes 262176 | tf_op jit(solution)/shard_map/all_to_all | solution.py:82
  102.1 3.6 %all-to-all-start.4 = ((bf16[4,512,384]{2,1,0:T(8,128)(2,1)}), bf16[4,512,384]{2,1,0:T(8,128)(2,1)S(1)}, u32[]{:S(2)}, u32[]{:S(2)}) async-start(bf16[4,512,384]{2,1,0:T(8,128)(2,1)} %bitcast.67), calls=%async_computation.4 | async-start | bytes 3145728 | tf_op jit(solution)/shard_map/all_to_all | solution.py:112
  105.7 1.8 convolution_convert_fusion
  107.4 18.3 %all-to-all-done.4 = bf16[4,512,384]{2,1,0:T(8,128)(2,1)S(1)} async-done(((bf16[4,512,384]{2,1,0:T(8,128)(2,1)}), bf16[4,512,384]{2,1,0:T(8,128)(2,1)S(1)}, u32[]{:S(2)}, u32[]{:S(2)}) %all-to-all-start.4) | async-done | bytes 1572896 | tf_op jit(solution)/shard_map/all_to_all | solution.py:112
  125.7 4.3 %all-to-all-start.6 = ((bf16[4,512,384]{2,1,0:T(8,128)(2,1)}), bf16[4,512,384]{2,1,0:T(8,128)(2,1)}, u32[]{:S(2)}, u32[]{:S(2)}) async-start(bf16[4,512,384]{2,1,0:T(8,128)(2,1)} %bitcast.66), calls=%async_computation.6 | async-start | bytes 3145728 | tf_op jit(solution)/shard_map/all_to_all | solution.py:126
  130.1 1.8 convolution_convert_fusion.1
  131.8 18.4 %all-to-all-done.6 = bf16[4,512,384]{2,1,0:T(8,128)(2,1)} async-done(((bf16[4,512,384]{2,1,0:T(8,128)(2,1)}), bf16[4,512,384]{2,1,0:T(8,128)(2,1)}, u32[]{:S(2)}, u32[]{:S(2)}) %all-to-all-start.6) | async-done | bytes 1572896 | tf_op jit(solution)/shard_map/all_to_all | solution.py:126
  150.2 4.5 %all-to-all-start.5 = ((bf16[4,512,384]{2,1,0:T(8,128)(2,1)}), bf16[4,512,384]{2,1,0:T(8,128)(2,1)}, u32[]{:S(2)}, u32[]{:S(2)}) async-start(bf16[4,512,384]{2,1,0:T(8,128)(2,1)} %bitcast.65), calls=%async_computation.5 | async-start | bytes 3145728 | tf_op jit(solution)/shard_map/all_to_all | solution.py:119
  155.8 1.4 convolution_convert_fusion.4
  157.2 1.4 convolution_convert_fusion.3
  158.7 1.8 reduce_sum.78
  160.5 0.9 copy.52
  161.4 1.1 reduce_sum.76
  162.5 12.4 %all-to-all-done.5 = bf16[4,512,384]{2,1,0:T(8,128)(2,1)} async-done(((bf16[4,512,384]{2,1,0:T(8,128)(2,1)}), bf16[4,512,384]{2,1,0:T(8,128)(2,1)}, u32[]{:S(2)}, u32[]{:S(2)}) %all-to-all-start.5) | async-done | bytes 1572896 | tf_op jit(solution)/shard_map/all_to_all | solution.py:119
  174.8 2.5 %reduce_sum.77 = bf16[512,384]{1,0:T(8,128)(2,1)} reduce(bf16[4,512,384]{2,1,0:T(8,128)(2,1)} %all-to-all-done.5, bf16[]{:T(256)} %constant.50.clone.1), dimensions={0}, to_apply=%region_8.10 | reduce | flops 589824 | bytes 1966082 | tf_op jit(solution)/shard_map/reduce_sum | solution.py:135
  (42 shorter events, 5.4 us)
Async XLA Ops:
  7.2 4.3 %copy-start = (bf16[128,2048]{1,0:T(8,128)(2,1)S(1)}, bf16[128,2048]{1,0:T(8,128)(2,1)}, u32[]{:S(2)}) copy-start(bf16[128,2048]{1,0:T(8,128)(2,1)} %param.10) | copy-start | bytes 1572868
  7.2 25.2 %all-gather.4.cloned.1.call-start = ((), (), s32[]{:S(2)}) async-start(), calls=%async_computation.7 | async-start | bytes 1966080 | tf_op jit(solution)/shard_map/all_gather | solution.py:58
  7.9 45.3 %all-gather.6.cloned.1.call-start = ((), (), s32[]{:S(2)}) async-start(), calls=%async_computation.8 | async-start | bytes 1966080 | tf_op jit(solution)/shard_map/all_gather | solution.py:59
  8.7 65.8 %all-gather.8.cloned.1.call-start = ((), (), s32[]{:S(2)}) async-start(), calls=%async_computation.9 | async-start | bytes 1966080 | tf_op jit(solution)/shard_map/all_gather | solution.py:60
  10.9 1.3 copy-start.1
  28.9 26.1 %all-to-all-start.2 = ((bf16[4,16,2048]{2,1,0:T(8,128)(2,1)}), bf16[4,16,2048]{2,1,0:T(8,128)(2,1)S(1)}, u32[]{:S(2)}, u32[]{:S(2)}) async-start(bf16[4,16,2048]{2,1,0:T(8,128)(2,1)} %bitcast.10), calls=%async_computation.2 | async-start | bytes 524288 | tf_op jit(solution)/shard_map/all_to_all | solution.py:67
  74.5 2.1 %copy-start.2 = (bf16[1,384,2048]{2,1,0:T(8,128)(2,1)S(1)}, bf16[1,384,2048]{2,1,0:T(8,128)(2,1)}, u32[]{:S(2)}) copy-start(bf16[1,384,2048]{2,1,0:T(8,128)(2,1)} %all-gather.8.cloned.1.call-done) | copy-start | bytes 4718596
  77.7 6.7 %copy-start.3 = (bf16[1,2048,384]{2,1,0:T(8,128)(2,1)S(1)}, bf16[1,2048,384]{2,1,0:T(8,128)(2,1)}, u32[]{:S(2)}) copy-start(bf16[1,2048,384]{2,1,0:T(8,128)(2,1)} %all-gather.6.cloned.1.call-done) | copy-start | bytes 4718596
  77.7 14.0 %all-to-all-start.1 = ((bf16[4,16,2048]{2,1,0:T(8,128)(2,1)}), bf16[4,16,2048]{2,1,0:T(8,128)(2,1)S(1)}, u32[]{:S(2)}, u32[]{:S(2)}) async-start(bf16[4,16,2048]{2,1,0:T(8,128)(2,1)} %bitcast.8), calls=%async_computation.1 | async-start | bytes 524288 | tf_op jit(solution)/shard_map/all_to_all | solution.py:75
  91.8 10.3 %all-to-all-start.3 = ((bf16[4,16,2048]{2,1,0:T(8,128)(2,1)}), bf16[4,16,2048]{2,1,0:T(8,128)(2,1)S(1)}, u32[]{:S(2)}, u32[]{:S(2)}) async-start(bf16[4,16,2048]{2,1,0:T(8,128)(2,1)} %bitcast.12), calls=%async_computation.3 | async-start | bytes 524288 | tf_op jit(solution)/shard_map/all_to_all | solution.py:82
  102.1 23.6 %all-to-all-start.4 = ((bf16[4,512,384]{2,1,0:T(8,128)(2,1)}), bf16[4,512,384]{2,1,0:T(8,128)(2,1)S(1)}, u32[]{:S(2)}, u32[]{:S(2)}) async-start(bf16[4,512,384]{2,1,0:T(8,128)(2,1)} %bitcast.67), calls=%async_computation.4 | async-start | bytes 3145728 | tf_op jit(solution)/shard_map/all_to_all | solution.py:112
  125.7 24.5 %all-to-all-start.6 = ((bf16[4,512,384]{2,1,0:T(8,128)(2,1)}), bf16[4,512,384]{2,1,0:T(8,128)(2,1)}, u32[]{:S(2)}, u32[]{:S(2)}) async-start(bf16[4,512,384]{2,1,0:T(8,128)(2,1)} %bitcast.66), calls=%async_computation.6 | async-start | bytes 3145728 | tf_op jit(solution)/shard_map/all_to_all | solution.py:126
  150.2 4.6 %copy-start.4 = (s32[128,8]{0,1:T(8,128)S(1)}, s32[128,8]{0,1:T(8,128)}, u32[]{:S(2)}) copy-start(s32[128,8]{0,1:T(8,128)} %param.11) | copy-start | bytes 12292
  150.2 5.0 %copy-start.5 = (f32[128,8]{0,1:T(8,128)S(1)}, f32[128,8]{0,1:T(8,128)}, u32[]{:S(2)}) copy-start(f32[128,8]{0,1:T(8,128)} %param.12) | copy-start | bytes 12292
  150.2 24.6 %all-to-all-start.5 = ((bf16[4,512,384]{2,1,0:T(8,128)(2,1)}), bf16[4,512,384]{2,1,0:T(8,128)(2,1)}, u32[]{:S(2)}, u32[]{:S(2)}) async-start(bf16[4,512,384]{2,1,0:T(8,128)(2,1)} %bitcast.65), calls=%async_computation.5 | async-start | bytes 3145728 | tf_op jit(solution)/shard_map/all_to_all | solution.py:119
Sparse Core Ops, SparseCore 0:
  9.6 22.3 all-gather.3
  33.5 19.6 all-gather.5
  54.8 19.6 all-gather.7
where the time goes:
time: 185 us; the launch traced here: 184 us
  waiting for transfers between devices  101 us (55%)
  starting transfers between devices  24 us (13%)
  matrix products  18.5 us (10%)
  blocking collectives  15 us (8%)
  between operations  14 us (8%)
  other arithmetic  7.8 us (4%)
  local copies, waits for them, and re-layouts  3.77 us (2%)
    all_gather x1, waiting for transfers between devices, on_device(): lax.all_gather(w_down, 'dp', axis=2, tiled=True)  19.5 us
    all_gather x1, waiting for transfers between devices, on_device(): lax.all_gather(w_up, 'dp', axis=1, tiled=True)  19.1 us
    all_to_all x1, waiting for transfers between devices, on_device(): lax.all_to_all(local_down.reshape(dp_count, slice_width, hidden_width), '...  18.4 us
    all_to_all x1, waiting for transfers between devices, on_device(): lax.all_to_all(local_gate.reshape(dp_count, slice_width, hidden_width), '...  18.3 us
    all_to_all x1, blocking collectives, on_device(): lax.all_to_all(send_x, 'expert', split_axis=0, concat_axis=0, tiled=True)  15 us
    all_to_all x1, waiting for transfers between devices, on_device(): lax.all_to_all(local_up.reshape(dp_count, slice_width, hidden_width), 'dp...  12.4 us
    all_to_all x1, waiting for transfers between devices, on_device(): lax.all_to_all(expert_out.reshape(expert_count, capacity, model_width), '...  5.98 us
    dot_general x4, matrix products, dot_last(): lax.dot_general(left, right, (((1,), (1,)), ((), ())), preferred_element_...  5.78 us
  transfers between devices with their start and end apart: 9, of which 7 were waited for; matrix products, arithmetic and copies ran while one was open for 13% of the time, Pallas kernels for 0%

commit v1 on v0

--- a/solution.py
+++ b/solution.py
@@ -4,6 +4,18 @@
 from jax.sharding import PartitionSpec as P
 
 EXPERTS = 128
+
+
+def collect(array, axis, dim):
+    ways, here, lap = (lax.axis_size(axis), lax.axis_index(axis), array.shape[dim])
+    shape = [n * ways if d == dim else n for d, n in enumerate(array.shape)]
+    full = lax.dynamic_update_slice_in_dim(
+        jnp.zeros(shape, array.dtype), array, here * lap, axis=dim
+    )
+    for far in range(1, ways):
+        array = lax.ppermute(array, axis, [(d, (d + 1) % ways) for d in range(ways)])
+        full = lax.dynamic_update_slice_in_dim(full, array, (here - far) % ways * lap, axis=dim)
+    return full
 
 
 def dot_last(left, right):
@@ -56,7 +68,7 @@
     )
     gate_full, up_full, down_full = (
         lax.all_gather(w_gate, "dp", axis=1, tiled=True),
-        lax.all_gather(w_up, "dp", axis=1, tiled=True),
+        collect(w_up, "dp", 1),
         lax.all_gather(w_down, "dp", axis=2, tiled=True),
     )
     gate_full = gate_full[0]

time: 185 us -> 168 us (0.908)
  waiting for transfers between devices: 101 us -> 85.4 us
  blocking collectives: 15 us -> 0 us
  starting transfers between devices: 24 us -> 35.7 us
  local copies, waits for them, and re-layouts: 3.77 us -> 7.21 us
    all_gather x1, waiting for transfers between devices: 19.5 us -> 0.02 us  [on_device(): lax.all_gather(w_down, 'dp', axis=2, tiled=True)]
    all_gather x1 -> x0, waiting for transfers between devices: 19.1 us -> none  [on_device(): lax.all_gather(w_up, 'dp', axis=1, tiled=True)]
    all_to_all x1 -> x0, blocking collectives: 15 us -> none  [on_device(): lax.all_to_all(send_x, 'expert', split_axis=0, concat_axis=0, tiled=True)]
    all_gather x1, waiting for transfers between devices: 0.02 us -> 10.4 us  [on_device(): lax.all_gather(w_gate, 'dp', axis=1, tiled=True)]
    ppermute x0 -> x3, waiting for transfers between devices: none -> 7.46 us  [collect(): lax.ppermute(array, axis, [(d, (d + 1) % ways) for d in range(ways)])]
    all_to_all x0 -> x1, waiting for transfers between devices: none -> 6.49 us  [on_device(): lax.all_to_all(send_x, 'expert', split_axis=0, concat_axis=0, tiled=True)]
    all_to_all x0 -> x1, starting transfers between devices: none -> 4.89 us  [on_device(): lax.all_to_all(send_x, 'expert', split_axis=0, concat_axis=0, tiled=True)]
    ppermute x0 -> x3, starting transfers between devices: none -> 4.63 us  [collect(): lax.ppermute(array, axis, [(d, (d + 1) % ways) for d in range(ways)])]
  transfers between devices with their start and end apart: 9 -> 12, of which waited for: 7 -> 9; matrix products, arithmetic and copies ran while one was open for 13% -> 15% of each run, Pallas kernels for 0% -> 0%
where the time goes in v1:
time: 168 us; the launch traced here: 167 us
  waiting for transfers between devices  85.4 us (51%)
  starting transfers between devices  35.7 us (21%)
  matrix products  17 us (10%)
  between operations  14.3 us (9%)
  other arithmetic  7.89 us (5%)
  local copies, waits for them, and re-layouts  7.21 us (4%)
    all_to_all x1, waiting for transfers between devices, on_device(): lax.all_to_all(local_down.reshape(dp_count, slice_width, hidden_width), '...  18.4 us
    all_to_all x1, waiting for transfers between devices, on_device(): lax.all_to_all(local_gate.reshape(dp_count, slice_width, hidden_width), '...  18.3 us
    all_to_all x1, waiting for transfers between devices, on_device(): lax.all_to_all(local_up.reshape(dp_count, slice_width, hidden_width), 'dp...  12.4 us
    all_gather x1, waiting for transfers between devices, on_device(): lax.all_gather(w_gate, 'dp', axis=1, tiled=True)  10.4 us
    ppermute x3, waiting for transfers between devices, collect(): lax.ppermute(array, axis, [(d, (d + 1) % ways) for d in range(ways)])  7.46 us
    all_to_all x1, waiting for transfers between devices, on_device(): lax.all_to_all(send_x, 'expert', split_axis=0, concat_axis=0, tiled=True)  6.49 us
    all_to_all x1, waiting for transfers between devices, on_device(): lax.all_to_all(expert_out.reshape(expert_count, capacity, model_width), '...  5.98 us
    all_to_all x1, starting transfers between devices, on_device(): lax.all_to_all(send_dy, 'expert', split_axis=0, concat_axis=0, tiled=True)  5.68 us
  transfers between devices with their start and end apart: 12, of which 9 were waited for; matrix products, arithmetic and copies ran while one was open for 15% of the time, Pallas kernels for 0%

profile of v1, /device:TPU:0, one launch (start us, length us, event | category | flops | bytes accessed | tf_op | source)
XLA Modules:
  0.0 167.4 jit_solution(567033461593028954)
XLA Ops:
  12.4 3.8 %collective-permute-done = bf16[1,512,384]{2,1,0:T(8,128)(2,1)} collective-permute-done((bf16[1,512,384]{2,1,0:T(8,128)(2,1)}, bf16[1,512,384]{2,1,0:T(8,128)(2,1)}, u32[]{:S(2)}, u32[]{:S(2)}) %collective-permute-start) | collective-permute-done | bytes 393248 | tf_op jit(solution)/shard_map/ppermute | solution.py:16
  17.1 5.7 %all-to-all-start.2 = ((bf16[4,16,2048]{2,1,0:T(8,128)(2,1)}), bf16[4,16,2048]{2,1,0:T(8,128)(2,1)S(1)}, u32[]{:S(2)}, u32[]{:S(2)}) async-start(bf16[4,16,2048]{2,1,0:T(8,128)(2,1)} %bitcast.13), calls=%async_computation.2 | async-start | bytes 524288 | tf_op jit(solution)/shard_map/all_to_all | solution.py:79
  23.0 3.6 %collective-permute-done.1 = bf16[1,512,384]{2,1,0:T(8,128)(2,1)} collective-permute-done((bf16[1,512,384]{2,1,0:T(8,128)(2,1)}, bf16[1,512,384]{2,1,0:T(8,128)(2,1)}, u32[]{:S(2)}, u32[]{:S(2)}) %collective-permute-start.1) | collective-permute-done | bytes 393248 | tf_op jit(solution)/shard_map/ppermute | solution.py:16
  26.7 4.1 %collective-permute-start.2 = (bf16[1,512,384]{2,1,0:T(8,128)(2,1)}, bf16[1,512,384]{2,1,0:T(8,128)(2,1)S(1)}, u32[]{:S(2)}, u32[]{:S(2)}) collective-permute-start(bf16[1,512,384]{2,1,0:T(8,128)(2,1)} %collective-permute-done.1), channel_id=1, source_target_pairs={{0,1},{1,2},{2,3},{3,0},{4,5},{5,6},{6,7},{7,4},{8,9},{9,10},{10,1... | collective-permute-start | bytes 1179656 | tf_op jit(solution)/shard_map/ppermute | solution.py:16
  30.8 1.1 bitcast_dynamic-update-slice_fusion.2
  31.8 1.1 bitcast_dynamic-update-slice_fusion.1
  32.9 4.9 %all-to-all-start = ((bf16[4,16,2048]{2,1,0:T(8,128)(2,1)}), bf16[4,16,2048]{2,1,0:T(8,128)(2,1)S(1)}, u32[]{:S(2)}, u32[]{:S(2)}) async-start(bf16[4,16,2048]{2,1,0:T(8,128)(2,1)} %bitcast.3), calls=%async_computation | async-start | bytes 524288 | tf_op jit(solution)/shard_map/all_to_all | solution.py:78
  37.9 2.0 %fusion.1 = f32[64,384]{1,0:T(8,128)S(1)} fusion(bf16[64,2048]{1,0:T(8,128)(2,1)S(1)} %bitcast.73, bf16[1,384,2048]{2,1,0:T(8,128)(2,1)} %all-gather.5.cloned.1.call-done), kind=kOutput, calls=%fused_computation.10 | convolution fusion | flops 100663296 | bytes 1933312 | tf_op jit(solution)/shard_map/dot_general | solution.py:22
  39.9 6.5 %all-to-all-done = bf16[4,16,2048]{2,1,0:T(8,128)(2,1)S(1)} async-done(((bf16[4,16,2048]{2,1,0:T(8,128)(2,1)}), bf16[4,16,2048]{2,1,0:T(8,128)(2,1)S(1)}, u32[]{:S(2)}, u32[]{:S(2)}) %all-to-all-start) | async-done | bytes 262176 | tf_op jit(solution)/shard_map/all_to_all | solution.py:78
  46.4 10.4 %all-gather.3.cloned.1.call-done = bf16[1,2048,384]{2,1,0:T(8,128)(2,1)} async-done(((bf16[1,512,384]{2,1,0:T(8,128)(2,1)}), bf16[1,2048,384]{2,1,0:T(8,128)(2,1)}) %all-gather.3.cloned.1.call-update) | async-done | bytes 1572880 | tf_op jit(solution)/shard_map/all_gather | solution.py:70
  56.8 1.8 %fusion.6 = f32[64,384]{1,0:T(8,128)S(1)} fusion(bf16[64,2048]{1,0:T(8,128)(2,1)S(1)} %bitcast.64, bf16[1,2048,384]{2,1,0:T(8,128)(2,1)} %all-gather.3.cloned.1.call-done), kind=kOutput, calls=%fused_computation.15 | convolution fusion | flops 100663296 | bytes 1933312 | tf_op jit(solution)/shard_map/dot_general | solution.py:28
  60.0 1.1 convolution_convert_fusion.5
  61.1 4.6 %all-to-all-start.1 = ((bf16[4,16,2048]{2,1,0:T(8,128)(2,1)}), bf16[4,16,2048]{2,1,0:T(8,128)(2,1)S(1)}, u32[]{:S(2)}, u32[]{:S(2)}) async-start(bf16[4,16,2048]{2,1,0:T(8,128)(2,1)} %bitcast.11), calls=%async_computation.1 | async-start | bytes 524288 | tf_op jit(solution)/shard_map/all_to_all | solution.py:87
  65.7 2.0 %fusion.4 = f32[64,2048]{1,0:T(8,128)S(1)} fusion(bf16[64,384]{1,0:T(8,128)(2,1)S(1)} %get-tuple-element.28, bf16[1,2048,384]{2,1,0:T(8,128)(2,1)} %all-gather.3.cloned.1.call-done), kind=kOutput, calls=%fused_computation.13 | convolution fusion | flops 100663296 | bytes 2146304 | tf_op jit(solution)/shard_map/dot_general | solution.py:22
  67.7 1.3 fusion
  69.0 6.0 %all-to-all-done.1 = bf16[4,16,2048]{2,1,0:T(8,128)(2,1)S(1)} async-done(((bf16[4,16,2048]{2,1,0:T(8,128)(2,1)}), bf16[4,16,2048]{2,1,0:T(8,128)(2,1)S(1)}, u32[]{:S(2)}, u32[]{:S(2)}) %all-to-all-start.1) | async-done | bytes 262176 | tf_op jit(solution)/shard_map/all_to_all | solution.py:87
  75.0 3.4 %all-to-all-start.3 = ((bf16[4,16,2048]{2,1,0:T(8,128)(2,1)}), bf16[4,16,2048]{2,1,0:T(8,128)(2,1)S(1)}, u32[]{:S(2)}, u32[]{:S(2)}) async-start(bf16[4,16,2048]{2,1,0:T(8,128)(2,1)} %bitcast.15), calls=%async_computation.3 | async-start | bytes 524288 | tf_op jit(solution)/shard_map/all_to_all | solution.py:94
  78.4 1.8 %convolution_convert_fusion.2 = bf16[2048,384]{1,0:T(8,128)(2,1)} fusion(bf16[64,2048]{1,0:T(8,128)(2,1)S(1)} %bitcast.66, bf16[64,384]{1,0:T(8,128)(2,1)S(1)} %get-tuple-element.28), kind=kOutput, calls=%fused_computation.4 | convolution fusion | flops 101449728 | bytes 1884160 | tf_op jit(solution)/shard_map/sd,sf->df/dot_general | solution.py:114
  80.2 5.1 %all-to-all-done.3 = bf16[4,16,2048]{2,1,0:T(8,128)(2,1)S(1)} async-done(((bf16[4,16,2048]{2,1,0:T(8,128)(2,1)}), bf16[4,16,2048]{2,1,0:T(8,128)(2,1)S(1)}, u32[]{:S(2)}, u32[]{:S(2)}) %all-to-all-start.3) | async-done | bytes 262176 | tf_op jit(solution)/shard_map/all_to_all | solution.py:94
  85.3 3.6 %all-to-all-start.4 = ((bf16[4,512,384]{2,1,0:T(8,128)(2,1)}), bf16[4,512,384]{2,1,0:T(8,128)(2,1)S(1)}, u32[]{:S(2)}, u32[]{:S(2)}) async-start(bf16[4,512,384]{2,1,0:T(8,128)(2,1)} %bitcast.70), calls=%async_computation.4 | async-start | bytes 3145728 | tf_op jit(solution)/shard_map/all_to_all | solution.py:124
  88.9 1.8 %convolution_convert_fusion = bf16[2048,384]{1,0:T(8,128)(2,1)} fusion(bf16[64,2048]{1,0:T(8,128)(2,1)S(1)} %bitcast.74, bf16[64,384]{1,0:T(8,128)(2,1)S(1)} %get-tuple-element.29), kind=kOutput, calls=%fused_computation.2 | convolution fusion | flops 101449728 | bytes 1884160 | tf_op jit(solution)/shard_map/sd,sf->df/dot_general | solution.py:120
  90.7 18.3 %all-to-all-done.4 = bf16[4,512,384]{2,1,0:T(8,128)(2,1)S(1)} async-done(((bf16[4,512,384]{2,1,0:T(8,128)(2,1)}), bf16[4,512,384]{2,1,0:T(8,128)(2,1)S(1)}, u32[]{:S(2)}, u32[]{:S(2)}) %all-to-all-start.4) | async-done | bytes 1572896 | tf_op jit(solution)/shard_map/all_to_all | solution.py:124
  109.0 4.3 %all-to-all-start.6 = ((bf16[4,512,384]{2,1,0:T(8,128)(2,1)}), bf16[4,512,384]{2,1,0:T(8,128)(2,1)}, u32[]{:S(2)}, u32[]{:S(2)}) async-start(bf16[4,512,384]{2,1,0:T(8,128)(2,1)} %bitcast.69), calls=%async_computation.6 | async-start | bytes 3145728 | tf_op jit(solution)/shard_map/all_to_all | solution.py:138
  113.3 1.8 %convolution_convert_fusion.1 = bf16[2048,384]{1,0:T(8,128)(2,1)} fusion(bf16[64,2048]{1,0:T(8,128)(2,1)S(1)} %bitcast.67, bf16[64,384]{1,0:T(8,128)(2,1)S(1)} %get-tuple-element.27), kind=kOutput, calls=%fused_computation.3 | convolution fusion | flops 101449728 | bytes 1884160 | tf_op jit(solution)/shard_map/sd,sf->df/dot_general | solution.py:117
  115.1 18.4 %all-to-all-done.6 = bf16[4,512,384]{2,1,0:T(8,128)(2,1)} async-done(((bf16[4,512,384]{2,1,0:T(8,128)(2,1)}), bf16[4,512,384]{2,1,0:T(8,128)(2,1)}, u32[]{:S(2)}, u32[]{:S(2)}) %all-to-all-start.6) | async-done | bytes 1572896 | tf_op jit(solution)/shard_map/all_to_all | solution.py:138
  133.5 4.5 %all-to-all-start.5 = ((bf16[4,512,384]{2,1,0:T(8,128)(2,1)}), bf16[4,512,384]{2,1,0:T(8,128)(2,1)}, u32[]{:S(2)}, u32[]{:S(2)}) async-start(bf16[4,512,384]{2,1,0:T(8,128)(2,1)} %bitcast.68), calls=%async_computation.5 | async-start | bytes 3145728 | tf_op jit(solution)/shard_map/all_to_all | solution.py:131
  139.1 1.4 convolution_convert_fusion.4
  140.5 1.4 convolution_convert_fusion.3
  141.9 1.8 %reduce_sum.78 = bf16[512,384]{1,0:T(8,128)(2,1)S(1)} reduce(bf16[4,512,384]{2,1,0:T(8,128)(2,1)} %all-to-all-done.6, bf16[]{:T(256)} %constant.84.clone.1), dimensions={0}, to_apply=%region_9.11 | reduce | flops 589824 | bytes 1966082 | tf_op jit(solution)/shard_map/reduce_sum | solution.py:148
  144.7 1.1 reduce_sum.76
  145.7 12.4 %all-to-all-done.5 = bf16[4,512,384]{2,1,0:T(8,128)(2,1)} async-done(((bf16[4,512,384]{2,1,0:T(8,128)(2,1)}), bf16[4,512,384]{2,1,0:T(8,128)(2,1)}, u32[]{:S(2)}, u32[]{:S(2)}) %all-to-all-start.5) | async-done | bytes 1572896 | tf_op jit(solution)/shard_map/all_to_all | solution.py:131
  158.1 2.5 %reduce_sum.77 = bf16[512,384]{1,0:T(8,128)(2,1)} reduce(bf16[4,512,384]{2,1,0:T(8,128)(2,1)} %all-to-all-done.5, bf16[]{:T(256)} %constant.84.clone.1), dimensions={0}, to_apply=%region_8.10 | reduce | flops 589824 | bytes 1966082 | tf_op jit(solution)/shard_map/reduce_sum | solution.py:147
  (51 shorter events, 9.7 us)
Async XLA Ops:
  7.2 3.5 %copy-start = (bf16[128,2048]{1,0:T(8,128)(2,1)S(1)}, bf16[128,2048]{1,0:T(8,128)(2,1)}, u32[]{:S(2)}) copy-start(bf16[128,2048]{1,0:T(8,128)(2,1)} %param.10) | copy-start | bytes 1572868
  7.2 30.7 %all-gather.5.cloned.1.call-start = ((), (), s32[]{:S(2)}) async-start(), calls=%async_computation.8 | async-start | bytes 1966080 | tf_op jit(solution)/shard_map/all_gather | solution.py:72
  7.9 48.9 %all-gather.3.cloned.1.call-start = ((), (), s32[]{:S(2)}) async-start(), calls=%async_computation.7 | async-start | bytes 1966080 | tf_op jit(solution)/shard_map/all_gather | solution.py:70
  8.0 8.2 %collective-permute-start = (bf16[1,512,384]{2,1,0:T(8,128)(2,1)}, bf16[1,512,384]{2,1,0:T(8,128)(2,1)}, u32[]{:S(2)}, u32[]{:S(2)}) collective-permute-start(bf16[1,512,384]{2,1,0:T(8,128)(2,1)} %param.14), channel_id=1, source_target_pairs={{0,1},{1,2},{2,3},{3,0},{4,5},{5,6},{6,7},{7,4},{8,9},{9,10},{10,1... | collective-permute-start | bytes 1179656 | tf_op jit(solution)/shard_map/ppermute | solution.py:16
  10.1 1.3 copy-start.1
  12.3 10.6 %copy-start.3 = (bf16[1,512,384]{2,1,0:T(8,128)(2,1)S(1)}, bf16[1,512,384]{2,1,0:T(8,128)(2,1)}, u32[]{:S(2)}) copy-start(bf16[1,512,384]{2,1,0:T(8,128)(2,1)} %param.14) | copy-start | bytes 1179652
  16.2 10.5 %collective-permute-start.1 = (bf16[1,512,384]{2,1,0:T(8,128)(2,1)}, bf16[1,512,384]{2,1,0:T(8,128)(2,1)}, u32[]{:S(2)}, u32[]{:S(2)}) collective-permute-start(bf16[1,512,384]{2,1,0:T(8,128)(2,1)} %collective-permute-done), channel_id=1, source_target_pairs={{0,1},{1,2},{2,3},{3,0},{4,5},{5,6},{6,7},{7,4},{8,9},{9,10},{10,1... | collective-permute-start | bytes 1179656 | tf_op jit(solution)/shard_map/ppermute | solution.py:16
  17.1 15.8 %all-to-all-start.2 = ((bf16[4,16,2048]{2,1,0:T(8,128)(2,1)}), bf16[4,16,2048]{2,1,0:T(8,128)(2,1)S(1)}, u32[]{:S(2)}, u32[]{:S(2)}) async-start(bf16[4,16,2048]{2,1,0:T(8,128)(2,1)} %bitcast.13), calls=%async_computation.2 | async-start | bytes 524288 | tf_op jit(solution)/shard_map/all_to_all | solution.py:79
  26.7 11.2 %collective-permute-start.2 = (bf16[1,512,384]{2,1,0:T(8,128)(2,1)}, bf16[1,512,384]{2,1,0:T(8,128)(2,1)S(1)}, u32[]{:S(2)}, u32[]{:S(2)}) collective-permute-start(bf16[1,512,384]{2,1,0:T(8,128)(2,1)} %collective-permute-done.1), channel_id=1, source_target_pairs={{0,1},{1,2},{2,3},{3,0},{4,5},{5,6},{6,7},{7,4},{8,9},{9,10},{10,1... | collective-permute-start | bytes 1179656 | tf_op jit(solution)/shard_map/ppermute | solution.py:16
  32.9 13.5 %all-to-all-start = ((bf16[4,16,2048]{2,1,0:T(8,128)(2,1)}), bf16[4,16,2048]{2,1,0:T(8,128)(2,1)S(1)}, u32[]{:S(2)}, u32[]{:S(2)}) async-start(bf16[4,16,2048]{2,1,0:T(8,128)(2,1)} %bitcast.3), calls=%async_computation | async-start | bytes 524288 | tf_op jit(solution)/shard_map/all_to_all | solution.py:78
  58.6 1.4 copy-start.2
  61.1 13.9 %all-to-all-start.1 = ((bf16[4,16,2048]{2,1,0:T(8,128)(2,1)}), bf16[4,16,2048]{2,1,0:T(8,128)(2,1)S(1)}, u32[]{:S(2)}, u32[]{:S(2)}) async-start(bf16[4,16,2048]{2,1,0:T(8,128)(2,1)} %bitcast.11), calls=%async_computation.1 | async-start | bytes 524288 | tf_op jit(solution)/shard_map/all_to_all | solution.py:87
  75.0 10.3 %all-to-all-start.3 = ((bf16[4,16,2048]{2,1,0:T(8,128)(2,1)}), bf16[4,16,2048]{2,1,0:T(8,128)(2,1)S(1)}, u32[]{:S(2)}, u32[]{:S(2)}) async-start(bf16[4,16,2048]{2,1,0:T(8,128)(2,1)} %bitcast.15), calls=%async_computation.3 | async-start | bytes 524288 | tf_op jit(solution)/shard_map/all_to_all | solution.py:94
  85.3 23.6 %all-to-all-start.4 = ((bf16[4,512,384]{2,1,0:T(8,128)(2,1)}), bf16[4,512,384]{2,1,0:T(8,128)(2,1)S(1)}, u32[]{:S(2)}, u32[]{:S(2)}) async-start(bf16[4,512,384]{2,1,0:T(8,128)(2,1)} %bitcast.70), calls=%async_computation.4 | async-start | bytes 3145728 | tf_op jit(solution)/shard_map/all_to_all | solution.py:124
  109.0 24.5 %all-to-all-start.6 = ((bf16[4,512,384]{2,1,0:T(8,128)(2,1)}), bf16[4,512,384]{2,1,0:T(8,128)(2,1)}, u32[]{:S(2)}, u32[]{:S(2)}) async-start(bf16[4,512,384]{2,1,0:T(8,128)(2,1)} %bitcast.69), calls=%async_computation.6 | async-start | bytes 3145728 | tf_op jit(solution)/shard_map/all_to_all | solution.py:138
  133.5 4.6 %copy-start.4 = (s32[128,8]{0,1:T(8,128)S(1)}, s32[128,8]{0,1:T(8,128)}, u32[]{:S(2)}) copy-start(s32[128,8]{0,1:T(8,128)} %param.11) | copy-start | bytes 12292
  133.5 5.0 %copy-start.5 = (f32[128,8]{0,1:T(8,128)S(1)}, f32[128,8]{0,1:T(8,128)}, u32[]{:S(2)}) copy-start(f32[128,8]{0,1:T(8,128)} %param.12) | copy-start | bytes 12292
  133.5 24.6 %all-to-all-start.5 = ((bf16[4,512,384]{2,1,0:T(8,128)(2,1)}), bf16[4,512,384]{2,1,0:T(8,128)(2,1)}, u32[]{:S(2)}, u32[]{:S(2)}) async-start(bf16[4,512,384]{2,1,0:T(8,128)(2,1)} %bitcast.68), calls=%async_computation.5 | async-start | bytes 3145728 | tf_op jit(solution)/shard_map/all_to_all | solution.py:131
Sparse Core Ops, SparseCore 0:
  9.6 24.9 all-gather.4
  36.2 20.6 all-gather.2
